TPU v7x, 32 devices: a whole 2x2x4 slice. The times are simulated.
32 devices in a mesh: req: 4 (over z), head: 8 (over y, x, core).
Axes of the slice: x: 2, y: 2, z: 4, core: 2. Of those that a mesh axis runs over, the one named last changes fastest.
Arguments:
- hidden_in: bfloat16 [64, 1024], P(('req', 'head')), may hold values from -6 to 6
- lengths: int32 [64], P('req'), may hold values from 2 to 1024, as said below
- request_order: int32 [64], replicated, may hold values from 0 to 63, each once
- key_cache: bfloat16 [2, 64, 16, 64, 1024], P(None, 'req', 'head')
- value_cache: bfloat16 [2, 64, 16, 64, 1024], P(None, 'req', 'head'), may hold values from -6 to 6
- w_qkv: bfloat16 [2, 16, 1024, 192], P(None, 'head'), may hold values from -0.1875 to 0.1875
- w_out: bfloat16 [2, 16, 64, 1024], P(None, 'head'), may hold values from -0.1875 to 0.1875
- w_up: bfloat16 [2, 1024, 4096], P(None, None, ('req', 'head')), may hold values from -0.1875 to 0.1875
- bias_up: bfloat16 [2, 4096], P(None, ('req', 'head')), may hold values from -3 to 3
- w_down: bfloat16 [2, 1024, 4096], P(None, None, ('req', 'head')), may hold values from -0.09375 to 0.09375
- norm_gain: float32 [2, 2, 1024], replicated, may hold values from 0.1 to 1.9
- norm_bias: float32 [2, 2, 1024], replicated, may hold values from -3 to 3
- embedding: bfloat16 [49152, 1024], P(('req', 'head')), may hold values from -0.59765625 to 0.59765625
Outputs:
- logits: float32 [64, 49152], P(None, ('req', 'head'))
Inputs may be any that keep to these rules, and one draw needn't show every extreme that they name: `lengths`: the largest length is 1024. Slot s of the caches and of lengths belongs to request request_order[s]; each request once.
All inputs are finite; a program needn't handle non-finite values.
Results may differ from a plain program's by a relative error of at most 0.0095.
Values may be sent and summed in bfloat16 or wider, within the bound.
A program may use at most 64 MiB of HBM per device.

v0:
```python
import jax
import jax.numpy as jnp
from jax import lax
from jax.sharding import PartitionSpec as P

LAYERS = 2


def layer_norm(values, gain_vec, bias_vec):
    average = jnp.mean(values, axis=-1, keepdims=True)
    centred = values - average
    variance = jnp.mean(centred * centred, axis=-1, keepdims=True)
    return centred * lax.rsqrt(variance + 1e-05) * gain_vec + bias_vec


def body(
    hidden_in,
    lengths,
    request_order,
    key_cache,
    value_cache,
    w_qkv,
    w_out,
    w_up,
    bias_up,
    w_down,
    norm_gain,
    norm_bias,
    embedding,
):
    group_size = lengths.shape[0]
    row_share = hidden_in.shape[0]
    head_size = w_out.shape[2]
    score_scale = head_size ** (-0.5)
    positions = jnp.arange(key_cache.shape[-1], dtype=jnp.int32)
    valid = positions[None, None, :] < lengths[:, None, None]
    gathered = lax.all_gather(hidden_in, ("req", "head"), axis=0, tiled=True)
    slot_ids = lax.dynamic_slice_in_dim(
        request_order, lax.axis_index("req") * group_size, group_size, 0
    )
    group_rows = gathered[slot_ids]
    own_rows = lax.dynamic_slice_in_dim(
        group_rows, lax.axis_index("head") * row_share, row_share, 0
    )
    for layer_idx in range(LAYERS):
        if layer_idx > 0:
            group_rows = lax.all_gather(own_rows, "head", axis=0, tiled=True)
        projected = jnp.einsum(
            "rd,hde->rhe", group_rows, w_qkv[layer_idx], preferred_element_type=jnp.float32
        ).astype(jnp.bfloat16)
        query = projected[..., :head_size]
        own_key = projected[..., head_size : 2 * head_size]
        own_value = projected[..., 2 * head_size :]
        scores = (
            jnp.einsum(
                "rhd,rhdl->rhl", query, key_cache[layer_idx], preferred_element_type=jnp.float32
            )
            * score_scale
        )
        scores = jnp.where(valid, scores, -jnp.inf)
        own = (
            jnp.sum(query.astype(jnp.float32) * own_key.astype(jnp.float32), axis=-1) * score_scale
        )
        row_max = jnp.maximum(jnp.max(scores, axis=-1), own)
        expo = jnp.exp(scores - row_max[..., None])
        own_exp = jnp.exp(own - row_max)
        denom = jnp.sum(expo, axis=-1) + own_exp
        mixed = jnp.einsum(
            "rhl,rhdl->rhd",
            expo.astype(jnp.bfloat16),
            value_cache[layer_idx],
            preferred_element_type=jnp.float32,
        )
        mixed = mixed + own_exp.astype(jnp.bfloat16).astype(jnp.float32)[
            ..., None
        ] * own_value.astype(jnp.float32)
        head_out = (mixed / denom[..., None]).astype(jnp.bfloat16)
        out_weight = w_out[layer_idx]
        attn_out = lax.psum_scatter(
            jnp.einsum("rhd,hde->re", head_out, out_weight, preferred_element_type=jnp.float32),
            "head",
            scatter_dimension=0,
            tiled=True,
        )
        normed = layer_norm(
            own_rows.astype(jnp.float32) + attn_out,
            norm_gain[layer_idx, 0],
            norm_bias[layer_idx, 0],
        ).astype(jnp.bfloat16)
        up_local = w_up[layer_idx]
        bias_local = bias_up[layer_idx].astype(jnp.float32)
        down_local = w_down[layer_idx]
        pre_act = (
            jnp.dot(
                lax.all_gather(normed, ("req", "head"), axis=0, tiled=True),
                up_local,
                preferred_element_type=jnp.float32,
            )
            + bias_local
        )
        hidden = jax.nn.gelu(pre_act, approximate=False).astype(jnp.bfloat16)
        mlp_out = lax.psum_scatter(
            jnp.einsum("rf,df->rd", hidden, down_local, preferred_element_type=jnp.float32),
            ("req", "head"),
            scatter_dimension=0,
            tiled=True,
        )
        own_rows = layer_norm(
            normed.astype(jnp.float32) + mlp_out, norm_gain[layer_idx, 1], norm_bias[layer_idx, 1]
        ).astype(jnp.bfloat16)
    everything = lax.all_gather(own_rows, ("req", "head"), axis=0, tiled=True)
    inverse = (
        jnp.zeros_like(request_order)
        .at[request_order]
        .set(jnp.arange(request_order.shape[0], dtype=jnp.int32))
    )
    return jnp.dot(everything[inverse], embedding.T, preferred_element_type=jnp.float32)


def solution(mesh):
    placed = (
        P(("req", "head"), None),
        P("req"),
        P(),
        P(None, "req", "head", None, None),
        P(None, "req", "head", None, None),
        P(None, "head", None, None),
        P(None, "head", None, None),
        P(None, None, ("req", "head")),
        P(None, ("req", "head")),
        P(None, None, ("req", "head")),
        P(),
        P(),
        P(("req", "head"), None),
    )
    return jax.shard_map(
        body, mesh=mesh, in_specs=placed, out_specs=P(None, ("req", "head")), check_vma=False
    )
```

profile of v0, /device:TPU:0, one launch (start us, length us, event | category | flops | bytes accessed | tf_op | source)
XLA Modules:
  0.0 567.9 jit_solution(7226839117564876502)
XLA Ops:
  6.5 0.9 compare_select_fusion.2
  7.4 43.9 %all-gather = bf16[32,2,1024]{2,1,0:T(2,128)(2,1)S(1)} all-gather(bf16[1,2,1024]{2,1,0:T(2,128)(2,1)} %bitcast.134), channel_id=1, replica_groups=mesh['req'=4,'head'=8] {'req','head'}, dimensions={0}, use_global_device_ids=true | all-gather | bytes 135168 | tf_op jit(solution)/shard_map/all_gather | solution.py:37
  51.4 0.1 reshape.149
  51.4 0.6 gather_fusion
  52.0 1.5 convolution_convert_fusion.1
  53.5 0.2 multiply_reduce_fusion.1
  53.6 0.7 iota_compare_fusion
  54.4 2.9 fusion.6
  57.3 0.1 fusion.38
  57.4 0.2 fusion.34
  57.7 3.4 fusion.4
  61.0 0.9 convolution_bitcast_fusion.1
  62.1 0.6 dynamic-slice
  63.4 47.4 %all-reduce.9.cloned.1.call-done = f32[16,1024]{1,0:T(8,128)} async-done(((f32[16,1024]{1,0:T(8,128)}), f32[16,1024]{1,0:T(8,128)}) %all-reduce.9.cloned.1.call-update) | async-done | bytes 65552
  110.8 0.9 fusion.215
  111.7 1.0 multiply_reduce_fusion.5
  112.6 0.8 add_convert_fusion.3
  113.5 40.2 %all-gather.1 = bf16[32,2,1024]{2,1,0:T(2,128)(2,1)S(1)} all-gather(bf16[1,2,1024]{2,1,0:T(2,128)(2,1)S(1)} %bitcast.125), channel_id=1, replica_groups=mesh['req'=4,'head'=8] {'req','head'}, dimensions={0}, use_global_device_ids=true | all-gather | bytes 135168 | tf_op jit(solution)/shard_map/all_gather | solution.py:95
  153.7 0.1 reshape.151
  153.8 2.1 fusion.20
  156.0 121.3 %all-reduce.11.cloned.1.call-done = f32[64,1024]{1,0:T(8,128)} async-done(((f32[64,1024]{1,0:T(8,128)}), f32[64,1024]{1,0:T(8,128)}) %all-reduce.11.cloned.1.call-update) | async-done | bytes 262160
  277.3 0.9 fusion.212
  278.2 0.9 multiply_reduce_fusion.4
  279.1 0.8 add_convert_fusion.2
  280.0 9.0 %all-gather.2 = bf16[8,2,1024]{2,1,0:T(2,128)(2,1)S(1)} all-gather(bf16[1,2,1024]{2,1,0:T(2,128)(2,1)S(1)} %bitcast.123), channel_id=1, replica_groups=mesh['req'=4,'head'=8] {'head'}, dimensions={0}, use_global_device_ids=true | all-gather | bytes 36864 | tf_op jit(solution)/shard_map/all_gather | solution.py:47
  289.0 1.4 convolution_convert_fusion
  290.4 0.2 multiply_reduce_fusion
  290.6 2.9 fusion.2
  293.5 0.1 fusion.39
  293.6 0.2 fusion.36
  293.9 3.4 fusion
  297.2 0.9 convolution_bitcast_fusion
  298.3 0.8 scatter_custom_fusion
  299.1 50.7 %all-reduce.13.cloned.1.call-done = f32[16,1024]{1,0:T(8,128)} async-done(((f32[16,1024]{1,0:T(8,128)}), f32[16,1024]{1,0:T(8,128)}) %all-reduce.13.cloned.1.call-update) | async-done | bytes 65552
  349.8 0.9 fusion.213
  350.7 0.9 multiply_reduce_fusion.3
  351.6 0.8 add_convert_fusion.1
  352.5 40.2 %all-gather.3 = bf16[32,2,1024]{2,1,0:T(2,128)(2,1)S(1)} all-gather(bf16[1,2,1024]{2,1,0:T(2,128)(2,1)S(1)} %bitcast.124), channel_id=1, replica_groups=mesh['req'=4,'head'=8] {'req','head'}, dimensions={0}, use_global_device_ids=true | all-gather | bytes 135168 | tf_op jit(solution)/shard_map/all_gather | solution.py:95
  392.7 0.1 reshape.155
  392.7 2.1 fusion.16
  394.9 121.3 %all-reduce.15.cloned.1.call-done = f32[64,1024]{1,0:T(8,128)} async-done(((f32[64,1024]{1,0:T(8,128)}), f32[64,1024]{1,0:T(8,128)}) %all-reduce.15.cloned.1.call-update) | async-done | bytes 262160
  516.2 0.9 fusion.214
  517.1 0.9 multiply_reduce_fusion.2
  518.0 0.8 fusion.147
  518.9 39.9 %all-gather.4 = bf16[32,2,1024]{2,1,0:T(2,128)(2,1)S(1)} all-gather(bf16[1,2,1024]{2,1,0:T(2,128)(2,1)S(1)} %fusion.147), channel_id=1, replica_groups=mesh['req'=4,'head'=8] {'req','head'}, dimensions={0}, use_global_device_ids=true | all-gather | bytes 135168 | tf_op jit(solution)/shard_map/all_gather | solution.py:111
  558.8 0.1 reshape.157
  558.8 0.7 gather_fusion.1
  559.5 1.8 fusion.218
  (47 shorter events, 0.4 us)
Async XLA Ops:
  6.5 553.0 %copy-start = (bf16[1536,1024]{1,0:T(8,128)(2,1)S(1)}, bf16[1536,1024]{1,0:T(8,128)(2,1)}, u32[]{:S(2)}) copy-start(bf16[1536,1024]{1,0:T(8,128)(2,1)} %param.25) | copy-start | bytes 9437188
  6.5 104.2 %all-reduce.9.cloned.1.call-start = ((), (), s32[]{:S(2)}) async-start(), calls=%async_computation | async-start | bytes 131072
  54.4 6.7 %copy-start.4 = (bf16[2,2,64,1024]{3,2,1,0:T(8,128)(2,1)S(1)}, bf16[2,2,64,1024]{3,2,1,0:T(8,128)(2,1)}, u32[]{:S(2)}) copy-start(bf16[2,2,64,1024]{3,2,1,0:T(8,128)(2,1)} %param.19) | copy-start | bytes 1572868
  54.4 7.7 %copy-start.1 = (f32[2,2,1024]{2,1,0:T(2,128)S(1)}, f32[2,2,1024]{2,1,0:T(2,128)}, u32[]{:S(2)}) copy-start(f32[2,2,1024]{2,1,0:T(2,128)} %param.23) | copy-start | bytes 49156
  54.4 7.7 %copy-start.2 = (f32[2,2,1024]{2,1,0:T(2,128)S(1)}, f32[2,2,1024]{2,1,0:T(2,128)}, u32[]{:S(2)}) copy-start(f32[2,2,1024]{2,1,0:T(2,128)} %param.24) | copy-start | bytes 49156
  54.4 7.7 %copy-start.3 = (bf16[2,128]{1,0:T(2,128)(2,1)S(1)}, bf16[2,128]{1,0:T(2,128)(2,1)}, u32[]{:S(2)}) copy-start(bf16[2,128]{1,0:T(2,128)(2,1)} %param.21) | copy-start | bytes 1540
  54.4 7.7 %copy-start.7 = (u32[32]{0:T(128)S(1)}, u32[32]{0:T(128)}, u32[]{:S(2)}) copy-start(u32[32]{0:T(128)} %constant.105) | copy-start | bytes 388
  62.0 215.3 %all-reduce.11.cloned.1.call-start = ((), (), s32[]{:S(2)}) async-start(), calls=%async_computation.1 | async-start | bytes 524288
  155.9 193.8 %all-reduce.13.cloned.1.call-start = ((), (), s32[]{:S(2)}) async-start(), calls=%async_computation.2 | async-start | bytes 131072
  290.6 6.6 %copy-start.5 = (bf16[2,2,64,1024]{3,2,1,0:T(8,128)(2,1)S(1)}, bf16[2,2,64,1024]{3,2,1,0:T(8,128)(2,1)}, u32[]{:S(2)}) copy-start(bf16[2,2,64,1024]{3,2,1,0:T(8,128)(2,1)} %param.19) | copy-start | bytes 1572868
  290.6 7.6 %copy-start.6 = (s32[64]{0:T(128)S(1)}, s32[64]{0:T(128)}, u32[]{:S(2)}) copy-start(s32[64]{0:T(128)} %param.15) | copy-start | bytes 772
  298.2 218.0 %all-reduce.15.cloned.1.call-start = ((), (), s32[]{:S(2)}) async-start(), calls=%async_computation.3 | async-start | bytes 524288
Sparse Core Ops, SparseCore 0:
  62.1 48.6 all-reduce.8
  156.0 121.1 all-reduce.10
  298.3 51.4 all-reduce.12
  395.0 121.1 all-reduce.14
where the time goes:
time: 569 us; the launch traced here: 568 us
  waiting for transfers between devices  341 us (60%)
  blocking collectives  173 us (30%)
  matrix products  23.4 us (4%)
  between operations  14 us (2%)
  other arithmetic  13.4 us (2%)
    unnamed x8, waiting for transfers between devices  341 us
    all_gather x2, blocking collectives, body(): lax.all_gather(normed, ('req', 'head'), axis=0, tiled=True)  80.5 us
    all_gather x1, blocking collectives, body(): gathered = lax.all_gather(hidden_in, ('req', 'head'), axis=0, tiled=True)  43.9 us
    all_gather x1, blocking collectives, body(): everything = lax.all_gather(own_rows, ('req', 'head'), axis=0, tiled=True)  39.9 us
  transfers between devices with their start and end apart: 4, of which 4 were waited for; matrix products, arithmetic and copies ran while one was open for 0% of the time, Pallas kernels for 0%

commit v1 on v0

--- a/solution.py
+++ b/solution.py
@@ -108,7 +108,14 @@
         own_rows = layer_norm(
             normed.astype(jnp.float32) + mlp_out, norm_gain[layer_idx, 1], norm_bias[layer_idx, 1]
         ).astype(jnp.bfloat16)
-    everything = lax.all_gather(own_rows, ("req", "head"), axis=0, tiled=True)
+    ways, here = (lax.axis_size(("req", "head")), lax.axis_index(("req", "head")))
+    everything, reach = (own_rows, 1)
+    while reach < ways:
+        theirs = lax.ppermute(everything, ("req", "head"), [(d, d ^ reach) for d in range(ways)])
+        mine_first = jnp.concatenate([everything, theirs], axis=0)
+        theirs_first = jnp.concatenate([theirs, everything], axis=0)
+        everything = jnp.where(here & reach == 0, mine_first, theirs_first)
+        reach = 2 * reach
     inverse = (
         jnp.zeros_like(request_order)
         .at[request_order]

time: 569 us -> 547 us (0.961)
  blocking collectives: 173 us -> 133 us
  waiting for transfers between devices: 341 us -> 353 us
  starting transfers between devices: 0.13 us -> 6.2 us
    all_gather x1 -> x0, blocking collectives: 39.9 us -> none  [body(): everything = lax.all_gather(own_rows, ('req', 'head'), axis=0, tiled=True)]
    ppermute x0 -> x5, waiting for transfers between devices: none -> 11.1 us  [body(): lax.ppermute(everything, ('req', 'head'), [(d, d ^ reach) for d in range(...]
    ppermute x0 -> x5, starting transfers between devices: none -> 6.07 us  [body(): lax.ppermute(everything, ('req', 'head'), [(d, d ^ reach) for d in range(...]
  transfers between devices with their start and end apart: 4 -> 9, of which waited for: 4 -> 9; matrix products, arithmetic and copies ran while one was open for 0% -> 0% of each run, Pallas kernels for 0% -> 0%
where the time goes in v1:
time: 547 us; the launch traced here: 546 us
  waiting for transfers between devices  353 us (65%)
  blocking collectives  133 us (24%)
  matrix products  23.4 us (4%)
  between operations  14 us (3%)
  other arithmetic  13.5 us (2%)
  starting transfers between devices  6.2 us (1%)
    unnamed x8, waiting for transfers between devices  342 us
    all_gather x2, blocking collectives, body(): lax.all_gather(normed, ('req', 'head'), axis=0, tiled=True)  80.5 us
    all_gather x1, blocking collectives, body(): gathered = lax.all_gather(hidden_in, ('req', 'head'), axis=0, tiled=True)  43.9 us
    ppermute x5, waiting for transfers between devices, body(): lax.ppermute(everything, ('req', 'head'), [(d, d ^ reach) for d in range(...  11.1 us
  transfers between devices with their start and end apart: 9, of which 9 were waited for; matrix products, arithmetic and copies ran while one was open for 0% of the time, Pallas kernels for 0%

profile of v1, /device:TPU:0, one launch (start us, length us, event | category | flops | bytes accessed | tf_op | source)
XLA Modules:
  0.0 546.0 jit_solution(4158055733513005439)
XLA Ops:
  6.5 0.9 compare_select_fusion.2
  7.4 43.9 %all-gather = bf16[32,2,1024]{2,1,0:T(2,128)(2,1)S(1)} all-gather(bf16[1,2,1024]{2,1,0:T(2,128)(2,1)} %bitcast.132), channel_id=1, replica_groups=mesh['req'=4,'head'=8] {'req','head'}, dimensions={0}, use_global_device_ids=true | all-gather | bytes 135168 | tf_op jit(solution)/shard_map/all_gather | solution.py:37
  51.4 0.6 gather_fusion
  52.0 1.5 convolution_convert_fusion.1
  53.6 0.7 iota_compare_fusion
  54.4 2.9 fusion.6
  57.4 0.2 fusion.34
  57.7 3.4 fusion.4
  61.0 0.9 convolution_bitcast_fusion.1
  62.1 0.6 dynamic-slice
  63.4 47.4 %all-reduce.9.cloned.1.call-done = f32[16,1024]{1,0:T(8,128)} async-done(((f32[16,1024]{1,0:T(8,128)}), f32[16,1024]{1,0:T(8,128)}) %all-reduce.9.cloned.1.call-update) | async-done | bytes 65552
  110.8 0.9 fusion.214
  111.7 1.0 multiply_reduce_fusion.5
  112.6 0.8 add_convert_fusion.3
  113.5 40.2 %all-gather.1 = bf16[32,2,1024]{2,1,0:T(2,128)(2,1)S(1)} all-gather(bf16[1,2,1024]{2,1,0:T(2,128)(2,1)S(1)} %bitcast.123), channel_id=1, replica_groups=mesh['req'=4,'head'=8] {'req','head'}, dimensions={0}, use_global_device_ids=true | all-gather | bytes 135168 | tf_op jit(solution)/shard_map/all_gather | solution.py:95
  153.8 2.1 fusion.20
  156.0 121.3 %all-reduce.11.cloned.1.call-done = f32[64,1024]{1,0:T(8,128)} async-done(((f32[64,1024]{1,0:T(8,128)}), f32[64,1024]{1,0:T(8,128)}) %all-reduce.11.cloned.1.call-update) | async-done | bytes 262160
  277.3 0.9 fusion.211
  278.2 0.9 multiply_reduce_fusion.4
  279.1 0.8 add_convert_fusion.2
  280.0 9.0 %all-gather.2 = bf16[8,2,1024]{2,1,0:T(2,128)(2,1)S(1)} all-gather(bf16[1,2,1024]{2,1,0:T(2,128)(2,1)S(1)} %bitcast.121), channel_id=1, replica_groups=mesh['req'=4,'head'=8] {'head'}, dimensions={0}, use_global_device_ids=true | all-gather | bytes 36864 | tf_op jit(solution)/shard_map/all_gather | solution.py:47
  289.0 1.4 convolution_convert_fusion
  290.6 2.9 fusion.2
  293.6 0.2 fusion.36
  293.9 3.4 fusion
  297.2 0.9 convolution_bitcast_fusion
  298.2 51.5 %all-reduce.13.cloned.1.call-done = f32[16,1024]{1,0:T(8,128)} async-done(((f32[16,1024]{1,0:T(8,128)}), f32[16,1024]{1,0:T(8,128)}) %all-reduce.13.cloned.1.call-update) | async-done | bytes 65552
  349.8 0.9 fusion.212
  350.7 0.9 multiply_reduce_fusion.3
  351.6 0.8 add_convert_fusion.1
  352.5 40.2 %all-gather.3 = bf16[32,2,1024]{2,1,0:T(2,128)(2,1)S(1)} all-gather(bf16[1,2,1024]{2,1,0:T(2,128)(2,1)S(1)} %bitcast.122), channel_id=1, replica_groups=mesh['req'=4,'head'=8] {'req','head'}, dimensions={0}, use_global_device_ids=true | all-gather | bytes 135168 | tf_op jit(solution)/shard_map/all_gather | solution.py:95
  392.7 2.1 fusion.16
  394.9 121.3 %all-reduce.15.cloned.1.call-done = f32[64,1024]{1,0:T(8,128)} async-done(((f32[64,1024]{1,0:T(8,128)}), f32[64,1024]{1,0:T(8,128)}) %all-reduce.15.cloned.1.call-update) | async-done | bytes 262160
  516.2 0.9 fusion.213
  517.1 0.9 multiply_reduce_fusion.2
  518.0 0.8 add_convert_fusion
  518.9 1.1 collective-permute-done
  520.1 1.5 collective-permute-start.1
  521.6 2.2 collective-permute-done.1
  523.9 1.5 collective-permute-start.2
  525.4 0.8 scatter_custom_fusion
  526.2 1.5 collective-permute-done.2
  527.7 1.5 collective-permute-start.3
  529.2 2.5 collective-permute-done.3
  531.7 1.5 collective-permute-start.4
  533.2 3.7 collective-permute-done.4
  536.9 0.7 gather_fusion.1
  537.6 1.8 fusion.217
  (60 shorter events, 1.3 us)
Async XLA Ops:
  6.5 531.1 %copy-start = (bf16[1536,1024]{1,0:T(8,128)(2,1)S(1)}, bf16[1536,1024]{1,0:T(8,128)(2,1)}, u32[]{:S(2)}) copy-start(bf16[1536,1024]{1,0:T(8,128)(2,1)} %param.25) | copy-start | bytes 9437188
  6.5 104.2 %all-reduce.9.cloned.1.call-start = ((), (), s32[]{:S(2)}) async-start(), calls=%async_computation | async-start | bytes 131072
  54.4 6.7 %copy-start.4 = (bf16[2,2,64,1024]{3,2,1,0:T(8,128)(2,1)S(1)}, bf16[2,2,64,1024]{3,2,1,0:T(8,128)(2,1)}, u32[]{:S(2)}) copy-start(bf16[2,2,64,1024]{3,2,1,0:T(8,128)(2,1)} %param.19) | copy-start | bytes 1572868
  54.4 7.7 %copy-start.1 = (f32[2,2,1024]{2,1,0:T(2,128)S(1)}, f32[2,2,1024]{2,1,0:T(2,128)}, u32[]{:S(2)}) copy-start(f32[2,2,1024]{2,1,0:T(2,128)} %param.23) | copy-start | bytes 49156
  54.4 7.7 %copy-start.2 = (f32[2,2,1024]{2,1,0:T(2,128)S(1)}, f32[2,2,1024]{2,1,0:T(2,128)}, u32[]{:S(2)}) copy-start(f32[2,2,1024]{2,1,0:T(2,128)} %param.24) | copy-start | bytes 49156
  54.4 7.7 %copy-start.3 = (bf16[2,128]{1,0:T(2,128)(2,1)S(1)}, bf16[2,128]{1,0:T(2,128)(2,1)}, u32[]{:S(2)}) copy-start(bf16[2,128]{1,0:T(2,128)(2,1)} %param.21) | copy-start | bytes 1540
  54.4 7.7 %copy-start.7 = (u32[32]{0:T(128)S(1)}, u32[32]{0:T(128)}, u32[]{:S(2)}) copy-start(u32[32]{0:T(128)} %constant.111) | copy-start | bytes 388
  62.0 215.3 %all-reduce.11.cloned.1.call-start = ((), (), s32[]{:S(2)}) async-start(), calls=%async_computation.1 | async-start | bytes 524288
  155.9 193.8 %all-reduce.13.cloned.1.call-start = ((), (), s32[]{:S(2)}) async-start(), calls=%async_computation.2 | async-start | bytes 131072
  290.6 6.6 %copy-start.5 = (bf16[2,2,64,1024]{3,2,1,0:T(8,128)(2,1)S(1)}, bf16[2,2,64,1024]{3,2,1,0:T(8,128)(2,1)}, u32[]{:S(2)}) copy-start(bf16[2,2,64,1024]{3,2,1,0:T(8,128)(2,1)} %param.19) | copy-start | bytes 1572868
  293.5 231.9 %copy-start.6 = (s32[64]{0:T(128)S(1)}, s32[64]{0:T(128)}, u32[]{:S(2)}) copy-start(s32[64]{0:T(128)} %param.15) | copy-start | bytes 772
  298.2 218.0 %all-reduce.15.cloned.1.call-start = ((), (), s32[]{:S(2)}) async-start(), calls=%async_computation.3 | async-start | bytes 524288
  518.9 1.2 collective-permute-start
  520.1 3.7 collective-permute-start.1
  523.9 3.8 collective-permute-start.2
  527.7 4.0 collective-permute-start.3
  531.7 5.2 collective-permute-start.4
Sparse Core Ops, SparseCore 0:
  62.1 48.6 all-reduce.8
  156.0 121.1 all-reduce.10
  298.3 51.4 all-reduce.12
  395.0 121.1 all-reduce.14
